TPU v7x, 32 devices: a whole 2x2x4 slice. The times are simulated.
32 devices in a mesh: sub: 4 (over y, x), row: 8 (over z, core).
Axes of the slice: x: 2, y: 2, z: 4, core: 2. Of those that a mesh axis runs over, the one named last changes fastest.
Arguments:
- inverse: float32 [4, 1024, 12288], P('sub', 'row')
- sources: float32 [4, 16, 12288], P('sub', None, 'row'), may hold values from -6 to 6
- line_history: float32 [4, 32, 1024], P('sub', None, 'row'), may hold values from -6 to 6
- line_dest: int32 [4, 1024], P('sub', 'row'), may hold values from 0 to 3, as said below
- line_port: int32 [4, 1024], P('sub', 'row'), may hold values from 0 to 1023
- line_delay: int32 [4, 1024], P('sub', 'row'), may hold values from 16 to 32
- prev_voltage: float32 [4, 1024], P('sub', 'row'), may hold values from -6 to 6
- flux_start: float32 [4, 1024], P('sub', 'row'), may hold values from -3 to 3
- arrester_gain: float32 [4, 1024], P('sub', 'row'), may hold values from 0.5 to 4
- core_gain: float32 [4, 1024], P('sub', 'row'), may hold values from 0.25 to 2
- arrester_slots: int32 [4, 128], P('sub', 'row'), may hold values from 0 to 127, as said below
- core_slots: int32 [4, 128], P('sub', 'row'), may hold values from 0 to 127, as said below
Outputs:
- voltages: float32 [4, 16, 1024], P('sub', None, 'row')
- final_flux: float32 [4, 1024], P('sub', 'row')
Inputs may be any that keep to these rules, and one draw needn't show every extreme that they name: `line_dest`: a record never names its own subnetwork; among the 128 records of one device no subnetwork is named more than 86 times, and in every such block some subnetwork is named exactly 86 times. `arrester_slots`: the 16 entries of one device are distinct slots of that device's 128 ports and share no slot with that device's core entries. `core_slots`: the 16 entries of one device are distinct slots of that device's 128 ports.
All inputs are finite; a program needn't handle non-finite values.
Results may differ from a plain program's by a relative error of at most 0.0003.
Values sent between devices are 32-bit elements; how exact they have to be, the bound alone decides.
A program may use at most 64 MiB of HBM per device.

v0:
```python
import jax
import jax.numpy as jnp
from jax import lax
from jax.sharding import PartitionSpec as P

STEPS = 16
HISTORY = 32
NEWTON = 2
half_step = 0.25
knee_volts = 1.5
cubic_term = 0.25


def element_terms(iterate, voltage, flux_now, arrester_mask, arrester_gain, core_mask, core_gain):
    linked = flux_now + half_step * (iterate + voltage)
    ratio = iterate / knee_volts
    current = arrester_mask * arrester_gain * iterate * (
        1.0 + ratio * ratio
    ) + core_mask * core_gain * (linked + cubic_term * linked * linked * linked)
    slope_now = arrester_mask * arrester_gain * (
        1.0 + 3.0 * ratio * ratio
    ) + core_mask * core_gain * half_step * (1.0 + 3.0 * cubic_term * linked * linked)
    return (current, slope_now)


def on_device(
    inverse,
    sources,
    line_history,
    line_dest,
    line_port,
    line_delay,
    prev_voltage,
    flux_start,
    arrester_gain,
    core_gain,
    arrester_slots,
    core_slots,
):
    matrix = inverse[0]
    port_rows = matrix.shape[0]
    row_count = lax.axis_size("row")
    slice_len = sources.shape[2]
    subnets = lax.axis_size("sub")
    lines_here = line_dest.shape[1]
    capacity = 2 * ((lines_here + subnets - 2) // (subnets - 1))
    target = line_dest[0]
    onehot_dest = (target[:, None] == jnp.arange(subnets, dtype=jnp.int32)[None, :]).astype(
        jnp.int32
    )
    running_rank = jnp.cumsum(onehot_dest, axis=0)
    within = jnp.sum(onehot_dest * running_rank, axis=1) - 1
    position = target * capacity + within
    placing = position[:, None] == jnp.arange(subnets * capacity, dtype=jnp.int32)[None, :]
    place_float = placing.astype(jnp.float32).reshape(lines_here, subnets, capacity)
    place_int = placing.astype(jnp.int32).reshape(lines_here, subnets, capacity)
    outgoing = jnp.einsum(
        "hl,lsc->shc", line_history[0], place_float, precision=lax.Precision.HIGHEST
    )
    port_slot = jnp.sum(place_int * (line_port[0] + 1)[:, None, None], axis=0) - 1
    delay_slot = jnp.sum(place_int * line_delay[0][:, None, None], axis=0)
    tag_block = jnp.stack([port_slot, delay_slot], axis=1)
    arrived, arrived_tags = (
        lax.all_to_all(outgoing, "sub", split_axis=0, concat_axis=0, tiled=True),
        lax.all_to_all(tag_block, "sub", split_axis=0, concat_axis=0, tiled=True),
    )
    records = subnets * capacity
    arrived_hist = jnp.transpose(arrived, (1, 0, 2)).reshape(HISTORY, records)
    arrived_port = arrived_tags[:, 0, :].reshape(records)
    arrived_delay = arrived_tags[:, 1, :].reshape(records)
    lag_index = HISTORY + jnp.arange(STEPS, dtype=jnp.int32)[:, None] - arrived_delay[None, :]
    lag_hit = jnp.arange(HISTORY, dtype=jnp.int32)[:, None, None] == lag_index[None, :, :]
    picked = jnp.sum(jnp.where(lag_hit, arrived_hist[:, None, :], 0.0), axis=0)
    landing = (
        arrived_port[:, None] == jnp.arange(row_count * port_rows, dtype=jnp.int32)[None, :]
    ).astype(jnp.float32)
    partial_value = -jnp.dot(picked, landing, precision=lax.Precision.HIGHEST)
    history = lax.psum_scatter(partial_value, "row", scatter_dimension=1, tiled=True)
    row_index = lax.axis_index("row")
    own_block = lax.dynamic_slice_in_dim(matrix, row_index * slice_len, port_rows, 1)
    self_imp = jnp.diagonal(own_block)
    arrest_here = arrester_gain[0]
    core_here = core_gain[0]
    source_rows = sources[0]
    window = jnp.concatenate(
        [source_rows[:, :port_rows] + history, source_rows[:, port_rows:]], axis=1
    )
    first_terms = lax.dot_general(
        lax.all_gather(window, "row", axis=1, tiled=True),
        matrix,
        (((1,), (1,)), ((), ())),
        precision=lax.Precision.HIGHEST,
    )
    coupling = matrix.reshape(port_rows, row_count, slice_len)[:, :, :port_rows].reshape(
        port_rows, row_count * port_rows
    )
    elem_slots = jnp.concatenate([arrester_slots[0], core_slots[0]])
    elem_count = elem_slots.shape[0]
    all_slots = lax.all_gather(elem_slots, "row", axis=0, tiled=True)
    global_ports = (
        jnp.arange(all_slots.shape[0], dtype=jnp.int32) // elem_count * port_rows + all_slots
    )
    cross_cols = jnp.take(coupling, global_ports, axis=1)
    own_rows = jnp.take(cross_cols, elem_slots, axis=0)
    arrest_flag = (jnp.arange(elem_count, dtype=jnp.int32) < arrester_slots.shape[1]).astype(
        jnp.float32
    )
    local_params = jnp.stack(
        [
            arrest_here[elem_slots],
            core_here[elem_slots],
            prev_voltage[0][elem_slots],
            flux_start[0][elem_slots],
            self_imp[elem_slots],
            arrest_flag,
        ],
        axis=1,
    )
    local_first = jnp.transpose(jnp.take(first_terms, elem_slots, axis=1))
    elem_matrix, elem_first, elem_params = (
        lax.all_gather(own_rows, "row", axis=0, tiled=True),
        lax.all_gather(local_first, "row", axis=0, tiled=True),
        lax.all_gather(local_params, "row", axis=0, tiled=True),
    )
    arrest_elem = elem_params[:, 0]
    core_elem = elem_params[:, 1]
    elem_self = elem_params[:, 4]
    elem_arrest = elem_params[:, 5]
    elem_core = 1.0 - elem_arrest

    def elem_advance(carried, first_now):
        voltage, flux_now = carried
        iterate = voltage
        current = jnp.zeros_like(voltage)
        for newton_pass in range(NEWTON):
            current, slope_now = element_terms(
                iterate, voltage, flux_now, elem_arrest, arrest_elem, elem_core, core_elem
            )
            network = first_now - jnp.dot(elem_matrix, current, precision=lax.Precision.HIGHEST)
            iterate = iterate - (iterate - network) / (1.0 + elem_self * slope_now)
        return ((iterate, flux_now + half_step * (iterate + voltage)), (iterate, current))

    (elem_last, elem_flux), (elem_volts, last_current) = lax.scan(
        elem_advance, (elem_params[:, 2], elem_params[:, 3]), jnp.transpose(elem_first)
    )
    own_volts = first_terms - lax.dot_general(
        last_current, cross_cols, (((1,), (1,)), ((), ())), precision=lax.Precision.HIGHEST
    )
    own_elem = lax.dynamic_slice_in_dim(elem_volts, row_index * elem_count, elem_count, 1)
    elem_place = (elem_slots[:, None] == jnp.arange(port_rows, dtype=jnp.int32)[None, :]).astype(
        jnp.float32
    )
    elem_here = jnp.sum(elem_place, axis=0)
    stacked = own_volts * (1.0 - elem_here) + jnp.dot(
        own_elem, elem_place, precision=lax.Precision.HIGHEST
    )
    previous = jnp.concatenate([prev_voltage[0][None, :], stacked[:-1]], axis=0)
    final_flux = flux_start[0] + half_step * jnp.sum(stacked + previous, axis=0)
    return (stacked[None], final_flux[None])


def solution(mesh):
    in_specs = (
        P("sub", "row", None),
        P("sub", None, "row"),
        P("sub", None, "row"),
        P("sub", "row"),
        P("sub", "row"),
        P("sub", "row"),
        P("sub", "row"),
        P("sub", "row"),
        P("sub", "row"),
        P("sub", "row"),
        P("sub", "row"),
        P("sub", "row"),
    )
    out_specs = (P("sub", None, "row"), P("sub", "row"))
    return jax.shard_map(
        on_device, mesh=mesh, in_specs=in_specs, out_specs=out_specs, check_vma=False
    )
```

profile of v0, /device:TPU:0, one launch (start us, length us, event | category | flops | bytes accessed | tf_op | source)
XLA Modules:
  0.0 157.2 jit_solution(13829604152136079206)
XLA Ops:
  7.2 0.7 fusion.25
  8.1 0.8 select_reduce_fusion.1
  8.9 0.7 add_add_fusion
  9.6 0.7 add_bitcast_fusion
  10.3 1.0 fusion.19
  11.2 0.6 pad_add_fusion
  11.8 5.2 %all-to-all-start = ((s32[4,2,86]{2,1,0:T(2,128)}), s32[4,2,86]{2,1,0:T(2,128)S(1)}, u32[]{:S(2)}, u32[]{:S(2)}) async-start(s32[4,2,86]{2,1,0:T(2,128)} %pad_add_fusion), calls=%async_computation | async-start | bytes 8192 | tf_op jit(solution)/shard_map/all_to_all | solution.py:65
  17.1 1.2 dynamic-slice.1
  19.0 0.8 fusion.36
  20.0 6.6 %copy.44 = f32[1,128,12288]{1,2,0:T(8,128)} copy(f32[1,128,12288]{2,1,0:T(8,128)} %param.14) | data formatting | bytes 12582912 | tf_op jit(solution)/shard_map/reshape;squeeze | solution.py:94
  26.6 0.9 dynamic-slice_bitcast_fusion
  27.6 1.2 gather_fusion.4
  28.8 0.7 gather_fusion.5
  29.5 0.7 gather_fusion
  30.2 0.7 gather_fusion.1
  30.9 0.7 gather_fusion.2
  31.6 0.7 gather_fusion.3
  32.4 14.3 %all-gather = f32[8,32,6]{1,2,0:T(8,128)S(1)} all-gather(f32[1,32,6]{1,2,0:T(8,128)S(1)} %bitcast.120), channel_id=1, replica_groups=mesh['sub'=4,'row'=8] {'row'}, dimensions={0}, use_global_device_ids=true | all-gather | bytes 6912 | tf_op jit(solution)/shard_map/all_gather | solution.py:123
  46.8 1.0 convolution_bitcast_fusion
  47.8 8.9 %all-reduce = s32[256]{0:T(256)S(1)} all-reduce(s32[256]{0:T(256)S(1)} %get-tuple-element.216), channel_id=1, replica_groups=mesh['sub'=4,'row'=8] {'row'}, use_global_device_ids=true, to_apply=%add | all-reduce | flops 256 | bytes 2048
  56.7 1.1 slice.75
  57.8 0.7 gather_fusion.7
  58.8 0.6 gather_fusion.8
  59.4 4.2 %all-to-all-start.1 = ((f32[4,32,86]{2,1,0:T(8,128)}), f32[4,32,86]{2,1,0:T(8,128)S(1)}, u32[]{:S(2)}, u32[]{:S(2)}) async-start(f32[4,32,86]{2,1,0:T(8,128)} %convolution_bitcast_fusion), calls=%async_computation.1 | async-start | bytes 131072 | tf_op jit(solution)/shard_map/all_to_all | solution.py:64
  63.9 4.6 %all-to-all-done.1 = f32[4,32,86]{2,1,0:T(8,128)S(1)} async-done(((f32[4,32,86]{2,1,0:T(8,128)}), f32[4,32,86]{2,1,0:T(8,128)S(1)}, u32[]{:S(2)}, u32[]{:S(2)}) %all-to-all-start.1) | async-done | bytes 44064 | tf_op jit(solution)/shard_map/all_to_all | solution.py:64
  68.7 1.2 fusion.15
  70.1 14.2 %all_gather.19 = f32[256,256]{1,0:T(8,128)S(1)} all-gather(f32[32,256]{1,0:T(8,128)S(1)} %broadcast_select_fusion), channel_id=1, replica_groups=mesh['sub'=4,'row'=8] {'row'}, dimensions={0}, use_global_device_ids=true | all-gather | bytes 294912 | tf_op jit(solution)/shard_map/all_gather | solution.py:121
  84.3 13.2 %reduce-scatter.2.cloned.1.call-done = f32[16,128]{1,0:T(8,128)} async-done(((f32[16,1024]{1,0:T(8,128)}), f32[16,128]{1,0:T(8,128)}) %reduce-scatter.2.cloned.1.call-update) | async-done | bytes 8208 | tf_op jit(solution)/shard_map/reduce_scatter | solution.py:78
  97.5 0.7 slice_add_fusion
  98.2 15.7 %all_gather.15 = f32[16,12288]{1,0:T(8,128)S(1)} all-gather(f32[16,1536]{1,0:T(8,128)S(1)} %pad_maximum_fusion), channel_id=1, replica_groups=mesh['sub'=4,'row'=8] {'row'}, dimensions={1}, use_global_device_ids=true | all-gather | bytes 884736 | tf_op jit(solution)/shard_map/all_gather | solution.py:89
  113.9 7.0 %fusion.12 = f32[16,128]{1,0:T(8,128)S(1)} fusion(f32[16,12288]{1,0:T(8,128)S(1)} %all_gather.15, f32[1,128,12288]{2,1,0:T(8,128)} %param.14), kind=kOutput, calls=%fused_computation.31 | convolution fusion | flops 301989888 | bytes 7086080 | tf_op jit(solution)/shard_map/dot_general | solution.py:88
  121.0 0.6 gather_fusion.6
  121.7 14.0 %all-gather.1 = f32[8,32,16]{1,2,0:T(8,128)S(1)} all-gather(f32[1,32,16]{1,2,0:T(8,128)S(1)} %copy.40), channel_id=1, replica_groups=mesh['sub'=4,'row'=8] {'row'}, dimensions={0}, use_global_device_ids=true | all-gather | bytes 18432 | tf_op jit(solution)/shard_map/all_gather | solution.py:122
  135.8 13.4 %while.19 = (s32[]{:T(128)}, f32[256]{0:T(256)S(1)}, f32[256]{0:T(256)S(1)}, f32[16,256]{1,0:T(8,128)S(1)}, f32[16,256]{1,0:T(8,128)S(1)}, /*index=5*/f32[16,256...) while((s32[]{:T(128)}, f32[256]{0:T(256)S(1)}, ...), condition=%wide.region_7.8_spmd, body=%wide.region_6.7_spmd.sunk | while | flops 1591042 | bytes 559233 | solution.py:143
  135.9 0.3 fusion.60
  136.2 0.3 fusion.62
  136.7 0.3 fusion.60
  137.1 0.3 fusion.62
  137.5 0.3 fusion.60
  137.9 0.3 fusion.62
  138.4 0.3 fusion.60
  138.7 0.3 fusion.62
  139.2 0.3 fusion.60
  139.6 0.3 fusion.62
  140.1 0.3 fusion.60
  140.4 0.3 fusion.62
  140.9 0.3 fusion.60
  141.3 0.3 fusion.62
  141.7 0.3 fusion.60
  142.1 0.3 fusion.62
  142.6 0.3 fusion.60
  142.9 0.3 fusion.62
  143.4 0.3 fusion.60
  143.8 0.3 fusion.62
  144.3 0.3 fusion.60
  144.6 0.3 fusion.62
  145.1 0.3 fusion.60
  145.5 0.3 fusion.62
  145.9 0.3 fusion.60
  146.3 0.3 fusion.62
  147.1 0.3 fusion.62
  148.0 0.3 fusion.62
  148.8 0.3 fusion.62
  149.8 0.5 bitcast_add_fusion
  (160 shorter events, 7.4 us)
Async XLA Ops:
  7.2 39.6 %copy-start = (f32[1,32,128]{2,1,0:T(8,128)S(1)}, f32[1,32,128]{2,1,0:T(8,128)}, u32[]{:S(2)}) copy-start(f32[1,32,128]{2,1,0:T(8,128)} %param.16) | copy-start | bytes 49156
  11.8 47.6 %all-to-all-start = ((s32[4,2,86]{2,1,0:T(2,128)}), s32[4,2,86]{2,1,0:T(2,128)S(1)}, u32[]{:S(2)}, u32[]{:S(2)}) async-start(s32[4,2,86]{2,1,0:T(2,128)} %pad_add_fusion), calls=%async_computation | async-start | bytes 8192 | tf_op jit(solution)/shard_map/all_to_all | solution.py:65
  19.9 7.6 %copy-start.7 = (s32[1,16]{1,0:T(1,128)S(1)}, s32[1,16]{1,0:T(1,128)}, u32[]{:S(2)}) copy-start(s32[1,16]{1,0:T(1,128)} %param.25) | copy-start | bytes 196
  19.9 7.6 %copy-start.8 = (s32[1,16]{1,0:T(1,128)S(1)}, s32[1,16]{1,0:T(1,128)}, u32[]{:S(2)}) copy-start(s32[1,16]{1,0:T(1,128)} %param.24) | copy-start | bytes 196
  19.9 9.6 %copy-start.2 = (f32[1,128]{1,0:T(1,128)S(1)}, f32[1,128]{1,0:T(1,128)}, u32[]{:S(2)}) copy-start(f32[1,128]{1,0:T(1,128)} %param.22) | copy-start | bytes 1540
  19.9 10.3 %copy-start.3 = (f32[1,128]{1,0:T(1,128)S(1)}, f32[1,128]{1,0:T(1,128)}, u32[]{:S(2)}) copy-start(f32[1,128]{1,0:T(1,128)} %param.23) | copy-start | bytes 1540
  19.9 11.0 %copy-start.1 = (f32[1,128]{1,0:T(1,128)S(1)}, f32[1,128]{1,0:T(1,128)}, u32[]{:S(2)}) copy-start(f32[1,128]{1,0:T(1,128)} %param.20) | copy-start | bytes 1540
  20.0 11.7 %copy-start.4 = (f32[1,128]{1,0:T(1,128)S(1)}, f32[1,128]{1,0:T(1,128)}, u32[]{:S(2)}) copy-start(f32[1,128]{1,0:T(1,128)} %param.21) | copy-start | bytes 1540
  26.6 43.5 %copy-start.5 = (f32[1,16,1536]{2,1,0:T(8,128)S(1)}, f32[1,16,1536]{2,1,0:T(8,128)}, u32[]{:S(2)}) copy-start(f32[1,16,1536]{2,1,0:T(8,128)} %param.15) | copy-start | bytes 294916
  59.4 9.0 %all-to-all-start.1 = ((f32[4,32,86]{2,1,0:T(8,128)}), f32[4,32,86]{2,1,0:T(8,128)S(1)}, u32[]{:S(2)}, u32[]{:S(2)}) async-start(f32[4,32,86]{2,1,0:T(8,128)} %convolution_bitcast_fusion), calls=%async_computation.1 | async-start | bytes 131072 | tf_op jit(solution)/shard_map/all_to_all | solution.py:64
  63.6 33.8 %reduce-scatter.2.cloned.1.call-start = ((), (), s32[]{:S(2)}) async-start(), calls=%async_computation.3 | async-start | bytes 73728 | tf_op jit(solution)/shard_map/reduce_scatter | solution.py:78
  149.7 0.6 copy-start.6
Sparse Core Ops, SparseCore 0:
  70.1 27.3 reduce-scatter.1
where the time goes:
time: 158 us; the launch traced here: 157 us
  blocking collectives  67.2 us (43%)
  local copies, waits for them, and re-layouts  19.8 us (13%)
  matrix products  18.1 us (11%)
  waiting for transfers between devices  17.8 us (11%)
  between operations  14.9 us (9%)
  other arithmetic  9.39 us (6%)
  starting transfers between devices  9.39 us (6%)
    all_gather x1, blocking collectives, on_device(): lax.all_gather(window, 'row', axis=1, tiled=True)  15.7 us
    all_gather x1, blocking collectives, on_device(): lax.all_gather(local_params, 'row', axis=0, tiled=True)  14.3 us
    all_gather x1, blocking collectives, on_device(): lax.all_gather(own_rows, 'row', axis=0, tiled=True)  14.2 us
    all_gather x1, blocking collectives, on_device(): lax.all_gather(local_first, 'row', axis=0, tiled=True)  14 us
    reduce_scatter x1, waiting for transfers between devices, on_device(): lax.psum_scatter(partial_value, 'row', scatter_dimension=1, tiled=True)  13.2 us
    unnamed x1, blocking collectives  8.92 us
    dot_general x32, matrix products, elem_advance(): jnp.dot(elem_matrix, current, precision=lax.Precision.HIGHEST)  8.45 us
    dot_general x1, matrix products, on_device(): lax.dot_general(lax.all_gather(window, 'row', axis=1, tiled=True), matrix...  6.97 us
  transfers between devices with their start and end apart: 3, of which 2 were waited for; matrix products, arithmetic and copies ran while one was open for 12% of the time, Pallas kernels for 0%

commit v1 on v0

--- a/solution.py
+++ b/solution.py
@@ -118,7 +118,9 @@
     )
     local_first = jnp.transpose(jnp.take(first_terms, elem_slots, axis=1))
     elem_matrix, elem_first, elem_params = (
-        lax.all_gather(own_rows, "row", axis=0, tiled=True),
+        jnp.concatenate(
+            lax.all_to_all(jnp.stack([own_rows] * lax.axis_size("row")), "row", 0, 0), axis=0
+        ),
         lax.all_gather(local_first, "row", axis=0, tiled=True),
         lax.all_gather(local_params, "row", axis=0, tiled=True),
     )

time: 158 us -> 166 us (1.051)
  waiting for transfers between devices: 17.8 us -> 36.2 us
  blocking collectives: 67.2 us -> 52.9 us
  starting transfers between devices: 9.39 us -> 12.8 us
    reduce_scatter x1, waiting for transfers between devices: 13.2 us -> 31.6 us  [on_device(): lax.psum_scatter(partial_value, 'row', scatter_dimension=1, tiled=True)]
    all_gather x1 -> x0, blocking collectives: 14.2 us -> none  [on_device(): lax.all_gather(own_rows, 'row', axis=0, tiled=True)]
    all_to_all x0 -> x1, starting transfers between devices: none -> 3.41 us  [on_device(): lax.all_to_all(jnp.stack([own_rows] * lax.axis_size('row')), 'row', 0, 0)]
  transfers between devices with their start and end apart: 3 -> 4, of which waited for: 2 -> 2; matrix products, arithmetic and copies ran while one was open for 12% -> 17% of each run, Pallas kernels for 0% -> 0%
where the time goes in v1:
time: 166 us
  blocking collectives  52.9 us (32%)
  waiting for transfers between devices  36.2 us (22%)
  local copies, waits for them, and re-layouts  20.5 us (12%)
  matrix products  18.1 us (11%)
  between operations  14.9 us (9%)
  starting transfers between devices  12.8 us (8%)
  other arithmetic  9.39 us (6%)
    reduce_scatter x1, waiting for transfers between devices, on_device(): lax.psum_scatter(partial_value, 'row', scatter_dimension=1, tiled=True)  31.6 us
    all_gather x1, blocking collectives, on_device(): lax.all_gather(window, 'row', axis=1, tiled=True)  15.7 us
    all_gather x1, blocking collectives, on_device(): lax.all_gather(local_params, 'row', axis=0, tiled=True)  14.3 us
    all_gather x1, blocking collectives, on_device(): lax.all_gather(local_first, 'row', axis=0, tiled=True)  14 us
    unnamed x1, blocking collectives  8.92 us
    dot_general x32, matrix products, elem_advance(): jnp.dot(elem_matrix, current, precision=lax.Precision.HIGHEST)  8.45 us
    dot_general x1, matrix products, on_device(): lax.dot_general(lax.all_gather(window, 'row', axis=1, tiled=True), matrix...  6.97 us
    another operation x1, local copies, waits for them, and re-layouts, on_device(): matrix.reshape(port_rows, row_count, slice_len)[:, :, :port_rows]  6.62 us
  transfers between devices with their start and end apart: 4, of which 2 were waited for; matrix products, arithmetic and copies ran while one was open for 17% of the time, Pallas kernels for 0%

profile of v1, /device:TPU:0, one launch (start us, length us, event | category | flops | bytes accessed | tf_op | source)
XLA Modules:
  0.0 165.6 jit_solution(4196994203992272681)
XLA Ops:
  7.2 0.7 fusion.25
  8.1 0.8 select_reduce_fusion.1
  8.9 0.7 add_add_fusion
  9.6 0.7 add_bitcast_fusion
  10.3 1.0 fusion.19
  11.2 0.6 pad_add_fusion
  11.8 5.2 %all-to-all-start = ((s32[4,2,86]{2,1,0:T(2,128)}), s32[4,2,86]{2,1,0:T(2,128)S(1)}, u32[]{:S(2)}, u32[]{:S(2)}) async-start(s32[4,2,86]{2,1,0:T(2,128)} %pad_add_fusion), calls=%async_computation | async-start | bytes 8192 | tf_op jit(solution)/shard_map/all_to_all | solution.py:65
  17.1 1.2 dynamic-slice.1
  19.0 0.8 fusion.36
  20.0 6.6 %copy.44 = f32[1,128,12288]{1,2,0:T(8,128)} copy(f32[1,128,12288]{2,1,0:T(8,128)} %param.14) | data formatting | bytes 12582912 | tf_op jit(solution)/shard_map/reshape;squeeze | solution.py:94
  26.6 0.9 dynamic-slice_bitcast_fusion
  27.6 1.2 gather_fusion.4
  28.8 0.7 gather_fusion.5
  29.5 0.7 gather_fusion
  30.2 0.7 gather_fusion.1
  30.9 0.7 gather_fusion.2
  31.6 0.7 gather_fusion.3
  32.4 14.3 %all-gather = f32[8,32,6]{1,2,0:T(8,128)S(1)} all-gather(f32[1,32,6]{1,2,0:T(8,128)S(1)} %bitcast.122), channel_id=1, replica_groups=mesh['sub'=4,'row'=8] {'row'}, dimensions={0}, use_global_device_ids=true | all-gather | bytes 6912 | tf_op jit(solution)/shard_map/all_gather | solution.py:125
  46.8 1.0 convolution_bitcast_fusion
  47.8 8.9 %all-reduce = s32[256]{0:T(256)S(1)} all-reduce(s32[256]{0:T(256)S(1)} %get-tuple-element.216), channel_id=1, replica_groups=mesh['sub'=4,'row'=8] {'row'}, use_global_device_ids=true, to_apply=%add | all-reduce | flops 256 | bytes 2048
  56.7 1.1 slice.75
  57.8 0.7 gather_fusion.7
  58.8 0.6 gather_fusion.8
  59.5 4.2 %all-to-all-start.1 = ((f32[4,32,86]{2,1,0:T(8,128)}), f32[4,32,86]{2,1,0:T(8,128)S(1)}, u32[]{:S(2)}, u32[]{:S(2)}) async-start(f32[4,32,86]{2,1,0:T(8,128)} %convolution_bitcast_fusion), calls=%async_computation.1 | async-start | bytes 131072 | tf_op jit(solution)/shard_map/all_to_all | solution.py:64
  63.9 4.6 %all-to-all-done.1 = f32[4,32,86]{2,1,0:T(8,128)S(1)} async-done(((f32[4,32,86]{2,1,0:T(8,128)}), f32[4,32,86]{2,1,0:T(8,128)S(1)}, u32[]{:S(2)}, u32[]{:S(2)}) %all-to-all-start.1) | async-done | bytes 44064 | tf_op jit(solution)/shard_map/all_to_all | solution.py:64
  68.5 0.7 stack.45
  69.2 3.4 %all-to-all-start.2 = ((f32[8,32,256]{2,1,0:T(8,128)}), f32[8,32,256]{2,1,0:T(8,128)S(1)}, u32[]{:S(2)}, u32[]{:S(2)}) async-start(f32[8,32,256]{2,1,0:T(8,128)} %stack.45), calls=%async_computation.3 | async-start | bytes 524288 | tf_op jit(solution)/shard_map/all_to_all | solution.py:122
  73.0 1.2 fusion.15
  74.2 31.6 %reduce-scatter.2.cloned.1.call-done = f32[16,128]{1,0:T(8,128)} async-done(((f32[16,1024]{1,0:T(8,128)}), f32[16,128]{1,0:T(8,128)}) %reduce-scatter.2.cloned.1.call-update) | async-done | bytes 8208 | tf_op jit(solution)/shard_map/reduce_scatter | solution.py:78
  105.9 0.7 slice_add_fusion
  106.6 15.7 %all_gather.12 = f32[16,12288]{1,0:T(8,128)S(1)} all-gather(f32[16,1536]{1,0:T(8,128)S(1)} %pad_maximum_fusion), channel_id=1, replica_groups=mesh['sub'=4,'row'=8] {'row'}, dimensions={1}, use_global_device_ids=true | all-gather | bytes 884736 | tf_op jit(solution)/shard_map/all_gather | solution.py:89
  122.3 7.0 %fusion.12 = f32[16,128]{1,0:T(8,128)S(1)} fusion(f32[16,12288]{1,0:T(8,128)S(1)} %all_gather.12, f32[1,128,12288]{2,1,0:T(8,128)} %param.14), kind=kOutput, calls=%fused_computation.31 | convolution fusion | flops 301989888 | bytes 7086080 | tf_op jit(solution)/shard_map/dot_general | solution.py:88
  129.4 0.6 gather_fusion.6
  130.1 14.0 %all-gather.1 = f32[8,32,16]{1,2,0:T(8,128)S(1)} all-gather(f32[1,32,16]{1,2,0:T(8,128)S(1)} %copy.40), channel_id=1, replica_groups=mesh['sub'=4,'row'=8] {'row'}, dimensions={0}, use_global_device_ids=true | all-gather | bytes 18432 | tf_op jit(solution)/shard_map/all_gather | solution.py:124
  144.2 13.4 %while.19 = (s32[]{:T(128)}, f32[256]{0:T(256)S(1)}, f32[256]{0:T(256)S(1)}, f32[16,256]{1,0:T(8,128)S(1)}, f32[16,256]{1,0:T(8,128)S(1)}, /*index=5*/f32[16,256...) while((s32[]{:T(128)}, f32[256]{0:T(256)S(1)}, ...), condition=%wide.region_7.8_spmd, body=%wide.region_6.7_spmd.sunk | while | flops 1591042 | bytes 559233 | solution.py:145
  144.2 0.3 fusion.60
  144.6 0.3 fusion.62
  145.1 0.3 fusion.60
  145.4 0.3 fusion.62
  145.9 0.3 fusion.60
  146.3 0.3 fusion.62
  146.8 0.3 fusion.60
  147.1 0.3 fusion.62
  148.0 0.3 fusion.62
  148.8 0.3 fusion.62
  149.6 0.3 fusion.62
  150.5 0.3 fusion.62
  151.0 0.3 fusion.60
  151.3 0.3 fusion.62
  151.8 0.3 fusion.60
  152.2 0.3 fusion.62
  152.6 0.3 fusion.60
  153.0 0.3 fusion.62
  153.5 0.3 fusion.60
  153.8 0.3 fusion.62
  154.3 0.3 fusion.60
  154.7 0.3 fusion.62
  155.1 0.3 fusion.60
  155.5 0.3 fusion.62
  156.0 0.3 fusion.60
  156.3 0.3 fusion.62
  156.8 0.3 fusion.60
  157.2 0.3 fusion.62
  158.1 0.5 bitcast_add_fusion
  (162 shorter events, 7.7 us)
Async XLA Ops:
  7.2 39.6 %copy-start = (f32[1,32,128]{2,1,0:T(8,128)S(1)}, f32[1,32,128]{2,1,0:T(8,128)}, u32[]{:S(2)}) copy-start(f32[1,32,128]{2,1,0:T(8,128)} %param.16) | copy-start | bytes 49156
  11.8 47.6 %all-to-all-start = ((s32[4,2,86]{2,1,0:T(2,128)}), s32[4,2,86]{2,1,0:T(2,128)S(1)}, u32[]{:S(2)}, u32[]{:S(2)}) async-start(s32[4,2,86]{2,1,0:T(2,128)} %pad_add_fusion), calls=%async_computation | async-start | bytes 8192 | tf_op jit(solution)/shard_map/all_to_all | solution.py:65
  19.9 7.6 %copy-start.7 = (s32[1,16]{1,0:T(1,128)S(1)}, s32[1,16]{1,0:T(1,128)}, u32[]{:S(2)}) copy-start(s32[1,16]{1,0:T(1,128)} %param.25) | copy-start | bytes 196
  19.9 7.6 %copy-start.8 = (s32[1,16]{1,0:T(1,128)S(1)}, s32[1,16]{1,0:T(1,128)}, u32[]{:S(2)}) copy-start(s32[1,16]{1,0:T(1,128)} %param.24) | copy-start | bytes 196
  19.9 9.6 %copy-start.2 = (f32[1,128]{1,0:T(1,128)S(1)}, f32[1,128]{1,0:T(1,128)}, u32[]{:S(2)}) copy-start(f32[1,128]{1,0:T(1,128)} %param.22) | copy-start | bytes 1540
  19.9 10.3 %copy-start.3 = (f32[1,128]{1,0:T(1,128)S(1)}, f32[1,128]{1,0:T(1,128)}, u32[]{:S(2)}) copy-start(f32[1,128]{1,0:T(1,128)} %param.23) | copy-start | bytes 1540
  19.9 11.0 %copy-start.1 = (f32[1,128]{1,0:T(1,128)S(1)}, f32[1,128]{1,0:T(1,128)}, u32[]{:S(2)}) copy-start(f32[1,128]{1,0:T(1,128)} %param.20) | copy-start | bytes 1540
  20.0 11.7 %copy-start.4 = (f32[1,128]{1,0:T(1,128)S(1)}, f32[1,128]{1,0:T(1,128)}, u32[]{:S(2)}) copy-start(f32[1,128]{1,0:T(1,128)} %param.21) | copy-start | bytes 1540
  26.6 32.9 %copy-start.5 = (f32[1,16,1536]{2,1,0:T(8,128)S(1)}, f32[1,16,1536]{2,1,0:T(8,128)}, u32[]{:S(2)}) copy-start(f32[1,16,1536]{2,1,0:T(8,128)} %param.15) | copy-start | bytes 294916
  59.5 9.0 %all-to-all-start.1 = ((f32[4,32,86]{2,1,0:T(8,128)}), f32[4,32,86]{2,1,0:T(8,128)S(1)}, u32[]{:S(2)}, u32[]{:S(2)}) async-start(f32[4,32,86]{2,1,0:T(8,128)} %convolution_bitcast_fusion), calls=%async_computation.1 | async-start | bytes 131072 | tf_op jit(solution)/shard_map/all_to_all | solution.py:64
  69.2 75.0 %all-to-all-start.2 = ((f32[8,32,256]{2,1,0:T(8,128)}), f32[8,32,256]{2,1,0:T(8,128)S(1)}, u32[]{:S(2)}, u32[]{:S(2)}) async-start(f32[8,32,256]{2,1,0:T(8,128)} %stack.45), calls=%async_computation.3 | async-start | bytes 524288 | tf_op jit(solution)/shard_map/all_to_all | solution.py:122
  72.7 33.2 %reduce-scatter.2.cloned.1.call-start = ((), (), s32[]{:S(2)}) async-start(), calls=%async_computation.4 | async-start | bytes 73728 | tf_op jit(solution)/shard_map/reduce_scatter | solution.py:78
  158.1 0.6 copy-start.6
Sparse Core Ops, SparseCore 0:
  75.7 30.1 reduce-scatter.1
